TPU v7x, 256 devices: a whole 4x4x8 slice. The times are simulated.
256 devices in a mesh: req: 32 (over z, y), mdl: 8 (over x, core).
Axes of the slice: x: 4, y: 4, z: 8, core: 2. Of those that a mesh axis runs over, the one named last changes fastest.
Arguments:
- stream: bfloat16 [24576, 1792], P('req'), may hold values from -6 to 6
- attention_projection_weight: bfloat16 [3, 1792, 1792], P(None, 'mdl'), may hold values from -0.125 to 0.125
- head_output_weight: bfloat16 [1792, 1792], P('mdl'), may hold values from -0.125 to 0.125
- adapter_down_maps: bfloat16 [64, 1792, 16], P('mdl'), may hold values from -0.125 to 0.125
- adapter_up_maps: bfloat16 [2, 1792, 1024], P(None, 'mdl'), may hold values from -1.5 to 1.5
- tenant_adapter_scale: float32 [4], replicated, may hold values from 0.5 to 2
- feedforward_norm_gain: bfloat16 [1792], replicated, may hold values from 0.099609375 to 1.8984375
- feedforward_weight: bfloat16 [3, 1792, 4864], P(None, 'req', 'mdl'), may hold values from -0.125 to 0.125
- prefix_cache_store: bfloat16 [1024, 2, 1792, 128], P('req', None, 'mdl'), may hold values from -140 to 140
- token_adapter_index: int32 [24576], P('req'), may hold values from 0 to 63
- request_token_lengths: int32 [32, 24], P('req'), may hold values from 1 to 192, 768 in all within a row
- request_tenant_index: int32 [768], P('req'), may hold values from 0 to 3
- last_page_holder: int32 [768, 1], replicated, may hold values from 0 to 31; in each aligned block of 24 rows (0 to 23, 24 to 47, ...) at most 2 rows name the same one
- holder_page_slot: int32 [768], replicated, may hold values from 0 to 31
- page_filled_rows: int32 [768], replicated, may hold values from 64 to 128
Outputs:
- layer_out: bfloat16 [24576, 1792], P(('req', 'mdl'))
Inputs may be any that keep to these rules, and one draw needn't show every extreme that they name: `last_page_holder`: within the rows of one index of req (aligned blocks of 24 rows) no holder is named more than 2 times, and one holder exactly 2 times in some blocks. `request_token_lengths`: each row sums to 768; its longest request has exactly 192 tokens.
All inputs are finite; a program needn't handle non-finite values.
Results may differ from a plain program's by a relative error of at most 0.025.
Values may be sent and summed in bfloat16 or wider, within the bound.
A program may use at most 128 MiB of HBM per device.

v0:
```python
import math
import jax
import jax.numpy as jnp
from jax import lax
from jax.sharding import PartitionSpec as P

HEAD_SIZE = 112
WINDOW = 64


def window_cols(one_page, fill_rows):
    return lax.dynamic_slice_in_dim(one_page, fill_rows - WINDOW, WINDOW, 2)


def per_device(
    stream,
    attention_projection_weight,
    head_output_weight,
    adapter_down_maps,
    adapter_up_maps,
    tenant_adapter_scale,
    feedforward_norm_gain,
    feedforward_weight,
    prefix_cache_store,
    token_adapter_index,
    request_token_lengths,
    request_tenant_index,
    last_page_holder,
    holder_page_slot,
    page_filled_rows,
):
    tok_count, model_width = stream.shape
    head_column_set = attention_projection_weight.shape[1]
    head_local = head_column_set // HEAD_SIZE
    req_per_dev = request_token_lengths.shape[1]
    rank_total_width = adapter_down_maps.shape[2]
    adapter_number = adapter_up_maps.shape[2] // rank_total_width
    req_devices = lax.axis_size("req")
    req_index = lax.axis_index("req")
    mdl_index = lax.axis_index("mdl")
    row_share = tok_count // lax.axis_size("mdl")
    cap_slots = max(2, (req_per_dev + req_devices - 1) // req_devices + 1)
    projected_rows = jnp.einsum(
        "td,kcd->ktc", stream, attention_projection_weight, preferred_element_type=jnp.float32
    )
    all_onehot = (
        token_adapter_index[:, None] == jnp.arange(adapter_number, dtype=jnp.int32)[None, :]
    )
    holder_count = adapter_down_maps.shape[0]
    holder_rank_rows = jnp.einsum(
        "qf,kfn->qkn", stream, adapter_down_maps, preferred_element_type=jnp.float32
    )
    held_onehot = (
        token_adapter_index[:, None]
        == (mdl_index * holder_count + jnp.arange(holder_count, dtype=jnp.int32))[None, :]
    )
    rank_part = jnp.sum(holder_rank_rows * held_onehot.astype(jnp.float32)[:, :, None], axis=1)
    rank_feat = lax.psum(rank_part.astype(jnp.bfloat16), "mdl")
    broadcast_result = (
        all_onehot.astype(jnp.bfloat16)[:, :, None] * rank_feat[:, None, :]
    ).reshape(tok_count, adapter_number * rank_total_width)
    adapter_column_set = jnp.einsum(
        "iu,pdu->ipd", broadcast_result, adapter_up_maps, preferred_element_type=jnp.float32
    )
    positions = jnp.arange(tok_count, dtype=jnp.int32)
    lengths_row = request_token_lengths[0]
    starts = jnp.cumsum(lengths_row) - lengths_row
    member = (positions[:, None] >= starts[None, :]) & (
        positions[:, None] < (starts + lengths_row)[None, :]
    )
    member_int = member.astype(jnp.int32)
    request_of = jnp.sum(member_int * jnp.arange(req_per_dev, dtype=jnp.int32)[None, :], axis=1)
    relative = positions - jnp.sum(member_int * starts[None, :], axis=1)
    tenant_hot = (
        request_tenant_index[:, None]
        == jnp.arange(tenant_adapter_scale.shape[0], dtype=jnp.int32)[None, :]
    ).astype(jnp.float32)
    request_scale = jnp.sum(tenant_hot * tenant_adapter_scale[None, :], axis=1)
    per_token_scale = jnp.sum(member.astype(jnp.float32) * request_scale[None, :], axis=1)[:, None]
    query_rows = (projected_rows[0] + per_token_scale * adapter_column_set[:, 0]).astype(
        jnp.bfloat16
    )
    key_rows = projected_rows[1].astype(jnp.bfloat16)
    value_row_block = (projected_rows[2] + per_token_scale * adapter_column_set[:, 1]).astype(
        jnp.bfloat16
    )
    owner_column = last_page_holder[:, 0]
    owner_table = owner_column.reshape(req_devices, req_per_dev)
    slot_table = holder_page_slot.reshape(req_devices, req_per_dev)
    owned = (owner_table == req_index).astype(jnp.int32)
    owned_rank = jnp.cumsum(owned, axis=1) - 1
    picked = owned[:, None, :] * (
        owned_rank[:, None, :] == jnp.arange(cap_slots, dtype=jnp.int32)[None, :, None]
    ).astype(jnp.int32)
    send_slot = jnp.sum(picked * slot_table[:, None, :], axis=2)
    my_owner = lax.dynamic_slice_in_dim(owner_column, req_index * req_per_dev, req_per_dev, 0)
    my_fill = lax.dynamic_slice_in_dim(page_filled_rows, req_index * req_per_dev, req_per_dev, 0)
    order_ids = jnp.arange(req_per_dev, dtype=jnp.int32)
    earlier = (my_owner[:, None] == my_owner[None, :]) & (order_ids[:, None] > order_ids[None, :])
    flat_pick = my_owner * cap_slots + jnp.sum(earlier.astype(jnp.int32), axis=1)
    source_pages = jnp.take(prefix_cache_store, send_slot, axis=0)
    page_inner = prefix_cache_store.shape[1:]
    arrived = lax.all_to_all(source_pages, "req", split_axis=0, concat_axis=0, tiled=True)
    chosen = jnp.take(arrived.reshape((req_devices * cap_slots,) + page_inner), flat_pick, axis=0)
    prefix_cols = jax.vmap(window_cols)(chosen, my_fill)
    prefix = jnp.transpose(prefix_cols, (0, 3, 1, 2))
    key_all = jnp.concatenate(
        [key_rows, prefix[:, :, 0].reshape(req_per_dev * WINDOW, head_column_set)], axis=0
    )
    value_all = jnp.concatenate(
        [value_row_block, prefix[:, :, 1].reshape(req_per_dev * WINDOW, head_column_set)], axis=0
    )
    distance = positions[:, None] - positions[None, :]
    local_ok = (request_of[:, None] == request_of[None, :]) & (distance >= 0) & (distance <= WINDOW)
    key_request = jnp.repeat(jnp.arange(req_per_dev, dtype=jnp.int32), WINDOW)
    key_offset = jnp.tile(jnp.arange(WINDOW, dtype=jnp.int32), req_per_dev)
    prefix_ok = (request_of[:, None] == key_request[None, :]) & (
        key_offset[None, :] >= relative[:, None]
    )
    allowed = jnp.concatenate([local_ok, prefix_ok], axis=1)
    query_heads = query_rows.reshape(tok_count, head_local, HEAD_SIZE)
    key_heads = key_all.reshape(-1, head_local, HEAD_SIZE)
    value_heads = value_all.reshape(-1, head_local, HEAD_SIZE)
    scores = jnp.einsum(
        "thd,shd->hts", query_heads, key_heads, preferred_element_type=jnp.float32
    ) * (1.0 / math.sqrt(HEAD_SIZE))
    masked = jnp.where(allowed[None], scores, -1e30)
    row_max = jnp.max(masked, axis=-1, keepdims=True)
    exp_scores = jnp.exp(masked - row_max)
    weights = (exp_scores / jnp.sum(exp_scores, axis=-1, keepdims=True)).astype(jnp.bfloat16)
    mixed = (
        jnp.einsum("hts,shd->thd", weights, value_heads, preferred_element_type=jnp.float32)
        .astype(jnp.bfloat16)
        .reshape(tok_count, head_column_set)
    )
    attn_part = (
        jnp.dot(mixed, head_output_weight, preferred_element_type=jnp.float32)
        .astype(jnp.bfloat16)
        .astype(jnp.float32)
    )
    gain_wide = feedforward_norm_gain.astype(jnp.float32)[None, :]
    attn_full = lax.psum(attn_part.astype(jnp.bfloat16), "mdl").astype(jnp.float32)
    resid_full = (stream.astype(jnp.float32) + attn_full).astype(jnp.bfloat16)
    resid_wide = resid_full.astype(jnp.float32)
    mean_sq = jnp.mean(resid_wide * resid_wide, axis=1, keepdims=True)
    normed = (resid_wide * lax.rsqrt(mean_sq + 1e-06) * gain_wide).astype(jnp.bfloat16)
    resid_mine = lax.dynamic_slice_in_dim(resid_full, mdl_index * row_share, row_share, 0)
    full_mlp = lax.all_gather(feedforward_weight, "req", axis=1, tiled=True)
    gate_part = jnp.dot(normed, full_mlp[0], preferred_element_type=jnp.float32)
    up_part = jnp.dot(normed, full_mlp[1], preferred_element_type=jnp.float32)
    hidden = (jax.nn.silu(gate_part) * up_part).astype(jnp.bfloat16)
    mlp_part = (
        jnp.einsum("tf,df->td", hidden, full_mlp[2], preferred_element_type=jnp.float32)
        .astype(jnp.bfloat16)
        .astype(jnp.float32)
    )
    mlp_mine = lax.psum_scatter(
        mlp_part.astype(jnp.bfloat16), "mdl", scatter_dimension=0, tiled=True
    ).astype(jnp.float32)
    return (resid_mine.astype(jnp.float32) + mlp_mine).astype(jnp.bfloat16)


def solution(mesh):
    return jax.shard_map(
        per_device,
        mesh=mesh,
        in_specs=(
            P("req", None),
            P(None, "mdl", None),
            P("mdl", None),
            P("mdl", None, None),
            P(None, "mdl", None),
            P(),
            P(),
            P(None, "req", "mdl"),
            P("req", None, "mdl", None),
            P("req"),
            P("req", None),
            P("req"),
            P(),
            P(),
            P(),
        ),
        out_specs=P(("req", "mdl"), None),
        check_vma=False,
    )
```

profile of v0, /device:TPU:8, one launch (start us, length us, event | category | flops | bytes accessed | tf_op | source)
XLA Modules:
  0.0 413.7 jit_solution(9208175052067111481)
XLA Ops:
  7.4 0.8 fusion.34
  8.2 0.1 reshape.176
  8.3 0.1 copy.31
  8.4 0.2 reduce_window_sum.18
  8.6 0.1 copy.30
  8.6 0.8 mul.153
  9.4 0.1 copy.32
  9.5 0.1 copy.34
  9.6 0.1 reshape.179
  9.8 0.1 copy.33
  9.9 6.5 %gather_fusion = bf16[64,2,224,128]{3,2,1,0:T(8,128)(2,1)} fusion(bf16[32,2,224,128]{3,2,1,0:T(8,128)(2,1)} %param.23, s32[1024]{0:T(1024)S(1)} %pad_clamp_fusion.1), kind=kCustom, calls=%fused_computation | custom fusion | bytes 14680320 | tf_op jit(solution)/shard_map/jit(_take)/gather | solution.py:101
  16.4 6.9 %broadcast_select_fusion = bf16[32,2,2,224,128]{4,3,2,1,0:T(8,128)(2,1)} fusion(bf16[32,2,2,224,128]{4,3,2,1,0:T(8,128)(2,1)} %bitcast.74, pred[32,2]{1,0:T(8,128)(4,1)S(1)} %copy.33), kind=kLoop, calls=%fused_computation.8 | loop fusion | flops 3670016 | bytes 14680128 | tf_op jit(solution)/shard_map/jit(_take)/select_n | solution.py:101
  23.2 11.9 %all-to-all-start = ((bf16[32,2,2,224,128]{4,3,2,1,0:T(8,128)(2,1)}), bf16[32,2,2,224,128]{4,3,2,1,0:T(8,128)(2,1)}, u32[]{:S(2)}, u32[]{:S(2)}) async-start(bf16[32,2,2,224,128]{4,3,2,1,0:T(8,128)(2,1)} %broadcast_select_fusion), calls=%async_computation | async-start | bytes 14680064 | tf_op jit(solution)/shard_map/all_to_all | solution.py:103
  35.1 0.0 all-reduce.3.cloned.1.call-start
  35.2 0.1 copy.28
  35.3 0.1 reduce
  35.4 0.1 eq.140
  35.5 0.1 ge.62
  35.6 3.9 fusion.17
  39.5 1.3 copy-done.2
  40.9 0.0 copy-start.10
  40.9 0.1 compare_convert_fusion
  41.0 2.8 fusion.50
  43.8 26.7 %psum.14 = bf16[768,16]{0,1:T(8,128)(2,1)S(1)} all-reduce(bf16[768,16]{0,1:T(8,128)(2,1)S(1)} %multiply_reduce_fusion), channel_id=1, replica_groups=mesh['req'=32,'mdl'=8] {'mdl'}, use_global_device_ids=true, to_apply=%region_4.5 | all-reduce | flops 12288 | bytes 49152 | tf_op jit(solution)/shard_map/psum | solution.py:58
  70.5 0.8 fusion.37
  71.3 0.2 convert_reduce_fusion
  71.5 0.8 and_bitcast_fusion
  72.3 0.1 select_reduce_fusion.3
  72.4 0.1 select_reduce_fusion.2
  72.5 0.1 select_reduce_fusion.1
  72.6 0.1 broadcast_multiply_fusion
  72.7 1.4 fusion.47
  74.1 2.1 fusion.51
  76.2 0.1 fusion.48
  76.3 0.3 fusion.14
  76.6 1.0 add_convert_fusion.3
  77.7 1.2 compare_and_fusion
  79.0 1.4 pad_add_fusion
  80.3 118.6 %all-to-all-done = bf16[32,2,2,224,128]{4,3,2,1,0:T(8,128)(2,1)} async-done(((bf16[32,2,2,224,128]{4,3,2,1,0:T(8,128)(2,1)}), bf16[32,2,2,224,128]{4,3,2,1,0:T(8,128)(2,1)}, u32[]{:S(2)}, u32[]{:S(2)}) %all-to-all-start) | async-done | bytes 7340064 | tf_op jit(solution)/shard_map/all_to_all | solution.py:103
  198.9 5.7 %gather_fusion.1 = bf16[24,2,224,128]{3,2,1,0:T(8,128)(2,1)} fusion(bf16[64,2,224,128]{3,2,1,0:T(8,128)(2,1)} %bitcast.16, s32[1024]{0:T(1024)S(1)} %pad_clamp_fusion), kind=kCustom, calls=%fused_computation.1 | custom fusion | bytes 5505120 | tf_op jit(solution)/shard_map/jit(_take)/gather | solution.py:104
  204.6 3.7 broadcast_select_fusion.1
  208.3 8.8 %copy.35 = bf16[24,2,224,128]{2,1,0,3:T(2,128)(2,1)} copy(bf16[24,2,224,128]{3,2,1,0:T(8,128)(2,1)} %broadcast_select_fusion.1) | data formatting | bytes 5505024 | tf_op jit(solution)/shard_map/jit(_take)/select_n | solution.py:104
  217.1 8.9 %gather_fusion.2 = bf16[24,2,224,64]{2,1,3,0:T(2,128)(2,1)S(1)} fusion(bf16[24,2,224,128]{2,1,0,3:T(2,128)(2,1)} %copy.35, s32[24]{0:T(128)S(1)} %get-tuple-element.21), kind=kCustom, calls=%fused_computation.2 | custom fusion | bytes 2752896 | tf_op jit(solution)/shard_map/vmap()/gather | solution.py:12
  226.0 6.5 %slice_reduce_fusion.1 = (bf16[24,64,224]{2,1,0:T(8,128)(2,1)S(1)}, bf16[24,64,224]{2,1,0:T(8,128)(2,1)S(1)}) fusion(bf16[24,64,2,224]{3,2,1,0:T(2,128)(2,1)S(1)} %bitcast.75), kind=kLoop, calls=%fused_computation.40 | loop fusion | bytes 2752512 | tf_op jit(solution)/shard_map/slice | solution.py:111
  232.5 0.4 concatenate.23
  232.9 0.6 copy.37
  233.5 0.4 concatenate.20
  233.9 0.6 copy.36
  234.5 0.0 copy-start.5
  234.5 9.7 %fusion.49 = (f32[2,768]{1,0:T(2,128)S(1)}, f32[2,768,2304]{2,1,0:T(8,128)}) fusion(pred[768,2304]{1,0:T(8,128)(4,1)} %pad_add_fusion, bf16[768,2,112]{0,2,1:T(8,128)(2,1)S(1)} %copy-done.6, bf16[1536,2,112]{0,2,1:T(8,128)(2,1)S(1)} %copy.37, bf16[768,2,112]{0,2,1:T(8,128)(2,1)S(1)} %bitcast.83), kind=kOutput, calls=%fused_computation.100 | convolution fusion | flops 808945920 | bytes 17307648 | tf_op jit(solution)/shard_map/sub | solution.py:129
  244.2 7.6 %fusion.22 = bf16[2,112,768]{2,1,0:T(8,128)(2,1)S(1)} fusion(f32[2,768,2304]{2,1,0:T(8,128)} %get-tuple-element.20, f32[2,768]{1,0:T(2,128)S(1)} %get-tuple-element.19, bf16[1536,2,112]{0,2,1:T(8,128)(2,1)S(1)} %copy.36, bf16[768,2,112]{0,2,1:T(8,128)(2,1)S(1)} %copy-done.5), kind=kOutput, calls=%fused_computation.41 | convolution fusion | flops 802037760 | bytes 15538176 | tf_op jit(solution)/shard_map/hts,shd->thd/dot_general | solution.py:132
  251.8 2.5 convolution_convert_fusion
  254.4 0.0 all-reduce.3.cloned.1.call-update
  254.4 0.0 all-gather.2.cloned.1.call-start
  254.4 0.5 all-gather.2.cloned.1.call-update
  255.0 0.0 reduce-scatter.2.cloned.1.call-start
  255.0 77.6 %all-reduce.3.cloned.1.call-done = bf16[768,1792]{1,0:T(8,128)(2,1)} async-done(((bf16[768,1792]{1,0:T(8,128)(2,1)}), bf16[768,1792]{1,0:T(8,128)(2,1)}) %all-reduce.3.cloned.1.call-update) | async-done | bytes 2752528 | tf_op jit(solution)/shard_map/psum | solution.py:142
  332.6 5.3 %fusion.6 = (f32[768]{0:T(1024)S(1)}, bf16[768,1792]{1,0:T(8,128)(2,1)}) fusion(bf16[768,1792]{1,0:T(8,128)(2,1)} %all-reduce.3.cloned.1.call-done, bf16[768,1792]{1,0:T(8,128)(2,1)} %param.15), kind=kLoop, calls=%fused_computation.16 | loop fusion | flops 9633024 | bytes 8260608 | tf_op jit(solution)/shard_map/reduce_sum | solution.py:145
  338.0 14.1 %all-gather.2.cloned.1.call-done = bf16[3,1792,608]{2,1,0:T(8,128)(2,1)} async-done(((bf16[3,56,608]{2,1,0:T(8,128)(2,1)}), bf16[3,1792,608]{2,1,0:T(8,128)(2,1)}) %all-gather.2.cloned.1.call-update) | async-done | bytes 6537232 | tf_op jit(solution)/shard_map/all_gather | solution.py:148
  352.0 5.8 %fusion.16 = f32[768,608]{0,1:T(8,128)} fusion(bf16[3,1792,608]{2,1,0:T(8,128)(2,1)} %all-gather.2.cloned.1.call-done, bf16[768,1792]{1,0:T(8,128)(2,1)} %get-tuple-element.10, f32[1792]{0:T(1024)S(1)} %convert_element_type.118, f32[768]{0:T(1024)S(1)} %add_rsqrt_fusion), kind=kOutput, calls=%fused_computation.35 | convolution fusion | flops 1679032320 | bytes 6924288 | tf_op jit(solution)/shard_map/dot_general | solution.py:149
  357.9 10.5 %convolution_convert_fusion.1 = bf16[768,1792]{1,0:T(8,128)(2,1)} fusion(bf16[3,1792,608]{2,1,0:T(8,128)(2,1)} %all-gather.2.cloned.1.call-done, f32[768,608]{0,1:T(8,128)} %fusion.16, bf16[768,1792]{1,0:T(8,128)(2,1)} %get-tuple-element.10, f32[1792]{0:T(1024)S(1)} %convert_element_type.118, f32[768]{0:T(1024)S(1)} %add_rsqrt_fusion), kind=kOutput, calls=%fused_computation.22 | convolution fusion | flops 3356737536 | bytes 11970560 | tf_op jit(solution)/shard_map/tf,df->td/dot_general | solution.py:153
  368.4 0.0 reduce-scatter.2.cloned.1.call-update
  368.5 36.0 %reduce-scatter.2.cloned.1.call-done = bf16[96,1792]{1,0:T(8,128)(2,1)} async-done(((bf16[768,1792]{1,0:T(8,128)(2,1)}), bf16[96,1792]{1,0:T(8,128)(2,1)}) %reduce-scatter.2.cloned.1.call-update) | async-done | bytes 344080 | tf_op jit(solution)/shard_map/reduce_scatter | solution.py:157
  404.4 1.9 add_convert_fusion.1
  (38 shorter events, 0.3 us)
Async XLA Ops:
  7.4 28.2 %copy-start = (bf16[3,224,1792]{2,1,0:T(8,128)(2,1)S(1)}, bf16[3,224,1792]{2,1,0:T(8,128)(2,1)}, u32[]{:S(2)}) copy-start(bf16[3,224,1792]{2,1,0:T(8,128)(2,1)} %param.16) | copy-start | bytes 7225348
  23.2 11.9 %copy-start.9 = (s32[1,24]{1,0:T(1,128)S(1)}, s32[1,24]{1,0:T(1,128)}, u32[]{:S(2)}) copy-start(s32[1,24]{1,0:T(1,128)} %param.25) | copy-start | bytes 292
  23.2 175.7 %all-to-all-start = ((bf16[32,2,2,224,128]{4,3,2,1,0:T(8,128)(2,1)}), bf16[32,2,2,224,128]{4,3,2,1,0:T(8,128)(2,1)}, u32[]{:S(2)}, u32[]{:S(2)}) async-start(bf16[32,2,2,224,128]{4,3,2,1,0:T(8,128)(2,1)} %broadcast_select_fusion), calls=%async_computation | async-start | bytes 14680064 | tf_op jit(solution)/shard_map/all_to_all | solution.py:103
  35.1 297.5 %all-reduce.3.cloned.1.call-start = ((), (), s32[]{:S(2)}) async-start(), calls=%async_computation.2 | async-start | bytes 5505024 | tf_op jit(solution)/shard_map/psum | solution.py:142
  35.6 5.3 %copy-start.7 = (s32[768]{0:T(1024)S(1)}, s32[768]{0:T(1024)}, u32[]{:S(2)}) copy-start(s32[768]{0:T(1024)} %param.24) | copy-start | bytes 9220
  35.6 5.4 %copy-start.4 = (bf16[8,1792,16]{1,2,0:T(8,128)(2,1)S(1)}, bf16[8,1792,16]{1,2,0:T(8,128)(2,1)}, u32[]{:S(2)}) copy-start(bf16[8,1792,16]{1,2,0:T(8,128)(2,1)} %param.18) | copy-start | bytes 1376260
  39.5 1.3 copy-start.2
  40.9 31.4 %copy-start.10 = (f32[4]{0:T(128)S(1)}, f32[4]{0:T(128)}, u32[]{:S(2)}) copy-start(f32[4]{0:T(128)} %param.20) | copy-start | bytes 52
  40.9 31.4 %copy-start.11 = (s32[24]{0:T(128)S(1)}, s32[24]{0:T(128)}, u32[]{:S(2)}) copy-start(s32[24]{0:T(128)} %param.26) | copy-start | bytes 292
  232.9 1.6 copy-start.6
  234.5 9.8 %copy-start.5 = (bf16[768,2,112]{0,2,1:T(8,128)(2,1)S(1)}, bf16[768,2,112]{0,2,1:T(8,128)(2,1)}, u32[]{:S(2)}) copy-start(bf16[768,2,112]{0,2,1:T(8,128)(2,1)} %get-tuple-element.17) | copy-start | bytes 1032196
  244.2 7.6 %copy-start.3 = (bf16[224,1792]{1,0:T(8,128)(2,1)S(1)}, bf16[224,1792]{1,0:T(8,128)(2,1)}, u32[]{:S(2)}) copy-start(bf16[224,1792]{1,0:T(8,128)(2,1)} %param.17) | copy-start | bytes 2408452
  251.8 3.2 copy-start.8
  254.4 97.6 %all-gather.2.cloned.1.call-start = ((), (), s32[]{:S(2)}) async-start(), calls=%async_computation.3 | async-start | bytes 7096320 | tf_op jit(solution)/shard_map/all_gather | solution.py:148
  255.0 149.4 %reduce-scatter.2.cloned.1.call-start = ((), (), s32[]{:S(2)}) async-start(), calls=%async_computation.4 | async-start | bytes 3096576 | tf_op jit(solution)/shard_map/reduce_scatter | solution.py:157
  357.9 48.4 %copy-start.1 = (bf16[3,224,1792]{2,1,0:T(8,128)(2,1)S(1)}, bf16[3,224,1792]{2,1,0:T(8,128)(2,1)}, u32[]{:S(2)}) copy-start(bf16[3,224,1792]{2,1,0:T(8,128)(2,1)} %param.16) | copy-start | bytes 7225348
Sparse Core Ops, SparseCore 0:
  254.5 78.0 all-reduce.2
  368.6 35.7 reduce-scatter.1
Sparse Core Ops, SparseCore 1:
  257.9 94.1 all-gather.1
where the time goes:
time: 415 us; the launch traced here: 414 us
  waiting for transfers between devices  247 us (60%)
  matrix products  45 us (11%)
  local copies, waits for them, and re-layouts  42.8 us (10%)
  blocking collectives  26.7 us (6%)
  other arithmetic  25.3 us (6%)
  between operations  15.2 us (4%)
  starting transfers between devices  12 us (3%)
    all_to_all x1, waiting for transfers between devices, per_device(): lax.all_to_all(source_pages, 'req', split_axis=0, concat_axis=0, tiled=True)  119 us
    psum x1, waiting for transfers between devices, per_device(): lax.psum(attn_part.astype(jnp.bfloat16), 'mdl').astype(jnp.float32)  77.6 us
    reduce_scatter x1, waiting for transfers between devices, per_device(): lax.psum_scatter(mlp_part.astype(jnp.bfloat16), 'mdl', scatter_dimension=...  36 us
    psum x1, blocking collectives, per_device(): rank_feat = lax.psum(rank_part.astype(jnp.bfloat16), 'mdl')  26.7 us
    all_gather x1, waiting for transfers between devices, per_device(): full_mlp = lax.all_gather(feedforward_weight, 'req', axis=1, tiled=True)  14.1 us
    all_to_all x1, starting transfers between devices, per_device(): lax.all_to_all(source_pages, 'req', split_axis=0, concat_axis=0, tiled=True)  11.9 us
    dot_general x1, matrix products, per_device(): jnp.einsum('tf,df->td', hidden, full_mlp[2], preferred_element_type=jnp.f...  10.5 us
    sub x1, matrix products, per_device(): exp_scores = jnp.exp(masked - row_max)  9.74 us
  transfers between devices with their start and end apart: 4, of which 4 were waited for; matrix products, arithmetic and copies ran while one was open for 5% of the time, Pallas kernels for 0%

commit v1 on v0

--- a/solution.py
+++ b/solution.py
@@ -145,7 +145,9 @@
     mean_sq = jnp.mean(resid_wide * resid_wide, axis=1, keepdims=True)
     normed = (resid_wide * lax.rsqrt(mean_sq + 1e-06) * gain_wide).astype(jnp.bfloat16)
     resid_mine = lax.dynamic_slice_in_dim(resid_full, mdl_index * row_share, row_share, 0)
-    full_mlp = lax.all_gather(feedforward_weight, "req", axis=1, tiled=True)
+    full_mlp = jnp.concatenate(
+        lax.all_to_all(jnp.stack([feedforward_weight] * lax.axis_size("req")), "req", 0, 0), axis=1
+    )
     gate_part = jnp.dot(normed, full_mlp[0], preferred_element_type=jnp.float32)
     up_part = jnp.dot(normed, full_mlp[1], preferred_element_type=jnp.float32)
     hidden = (jax.nn.silu(gate_part) * up_part).astype(jnp.bfloat16)

time: 415 us -> 440 us (1.060)
  blocking collectives: 26.7 us -> 200 us
  waiting for transfers between devices: 247 us -> 104 us
  local copies, waits for them, and re-layouts: 42.8 us -> 52.1 us
  starting transfers between devices: 12 us -> 5.83 us
  other arithmetic: 25.3 us -> 20.6 us
    all_to_all x0 -> x1, blocking collectives: none -> 175 us  [per_device(): lax.all_to_all(source_pages, 'req', split_axis=0, concat_axis=0, tiled=True)]
    all_to_all x1, waiting for transfers between devices: 119 us -> 50.1 us  [per_device(): lax.all_to_all(jnp.stack([feedforward_weight] * lax.axis_size('req')), 'r...]
    psum x1, waiting for transfers between devices: 77.6 us -> 16.4 us  [per_device(): lax.psum(attn_part.astype(jnp.bfloat16), 'mdl').astype(jnp.float32)]
    all_gather x1 -> x0, waiting for transfers between devices: 14.1 us -> none  [per_device(): full_mlp = lax.all_gather(feedforward_weight, 'req', axis=1, tiled=True)]
    all_to_all x1, starting transfers between devices: 11.9 us -> 5.75 us  [per_device(): lax.all_to_all(jnp.stack([feedforward_weight] * lax.axis_size('req')), 'r...]
    slice x0 -> x1, local copies, waits for them, and re-layouts: none -> 5.89 us  [per_device(): up_part = jnp.dot(normed, full_mlp[1], preferred_element_type=jnp.float32)]
  transfers between devices with their start and end apart: 4 -> 3, of which waited for: 4 -> 3; matrix products, arithmetic and copies ran while one was open for 5% -> 18% of each run, Pallas kernels for 0% -> 0%
where the time goes in v1:
time: 440 us; the launch traced here: 439 us
  blocking collectives  200 us (45%)
  waiting for transfers between devices  104 us (24%)
  local copies, waits for them, and re-layouts  52.1 us (12%)
  matrix products  42.6 us (10%)
  other arithmetic  20.6 us (5%)
  between operations  13.8 us (3%)
  starting transfers between devices  5.83 us (1%)
    all_to_all x1, blocking collectives, per_device(): lax.all_to_all(source_pages, 'req', split_axis=0, concat_axis=0, tiled=True)  175 us
    all_to_all x1, waiting for transfers between devices, per_device(): lax.all_to_all(jnp.stack([feedforward_weight] * lax.axis_size('req')), 'r...  50.1 us
    reduce_scatter x1, waiting for transfers between devices, per_device(): lax.psum_scatter(mlp_part.astype(jnp.bfloat16), 'mdl', scatter_dimension=...  37.3 us
    psum x1, blocking collectives, per_device(): rank_feat = lax.psum(rank_part.astype(jnp.bfloat16), 'mdl')  25.5 us
    psum x1, waiting for transfers between devices, per_device(): lax.psum(attn_part.astype(jnp.bfloat16), 'mdl').astype(jnp.float32)  16.4 us
    dot_general x1, matrix products, per_device(): jnp.einsum('tf,df->td', hidden, full_mlp[2], preferred_element_type=jnp.f...  10.6 us
    sub x1, matrix products, per_device(): exp_scores = jnp.exp(masked - row_max)  9.73 us
    gather x1, local copies, waits for them, and re-layouts, window_cols(): return lax.dynamic_slice_in_dim(one_page, fill_rows - WINDOW, WINDOW, 2)  8.89 us
  transfers between devices with their start and end apart: 3, of which 3 were waited for; matrix products, arithmetic and copies ran while one was open for 18% of the time, Pallas kernels for 0%

profile of v1, /device:TPU:8, one launch (start us, length us, event | category | flops | bytes accessed | tf_op | source)
XLA Modules:
  0.0 438.8 jit_solution(10670948626968024155)
XLA Ops:
  6.5 0.8 fusion.33
  7.4 0.1 reshape.189
  7.5 0.1 copy.31
  7.5 0.2 reduce_window_sum.18
  7.7 0.1 copy.30
  7.8 0.8 mul.153
  8.6 0.1 copy.32
  8.7 0.1 copy.34
  8.8 0.1 reshape.192
  8.9 0.1 copy.33
  9.0 6.5 %gather_fusion = bf16[64,2,224,128]{3,2,1,0:T(8,128)(2,1)} fusion(bf16[32,2,224,128]{3,2,1,0:T(8,128)(2,1)} %param.23, s32[1024]{0:T(1024)S(1)} %pad_clamp_fusion.1), kind=kCustom, calls=%fused_computation | custom fusion | bytes 14680320 | tf_op jit(solution)/shard_map/jit(_take)/gather | solution.py:101
  15.5 3.8 broadcast_select_fusion
  19.4 174.6 %all_to_all.10 = bf16[32,2,2,224,128]{4,3,2,1,0:T(8,128)(2,1)} all-to-all(bf16[32,2,2,224,128]{4,3,2,1,0:T(8,128)(2,1)S(1)} %broadcast_select_fusion), channel_id=1, replica_groups=mesh['req'=32,'mdl'=8] {'req'}, dimensions={0} | all-to-all | bytes 14680064 | tf_op jit(solution)/shard_map/all_to_all | solution.py:103
  194.0 3.4 stack.2
  197.4 5.7 %all-to-all-start.1 = ((bf16[32,3,56,608]{3,2,1,0:T(8,128)(2,1)}), bf16[32,3,56,608]{3,2,1,0:T(8,128)(2,1)}, u32[]{:S(2)}, u32[]{:S(2)}) async-start(bf16[32,3,56,608]{3,2,1,0:T(8,128)(2,1)} %stack.2), calls=%async_computation.1 | async-start | bytes 13762560 | tf_op jit(solution)/shard_map/all_to_all | solution.py:149
  203.2 0.0 all-reduce.3.cloned.1.call-start
  203.2 0.1 copy.28
  203.4 0.1 reduce
  203.5 0.1 eq.140
  203.6 0.1 ge.62
  203.7 3.9 fusion.15
  207.6 1.4 copy-done.3
  209.0 0.1 compare_convert_fusion
  209.1 2.8 fusion.50
  211.9 25.5 %psum.14 = bf16[768,16]{0,1:T(8,128)(2,1)S(1)} all-reduce(bf16[768,16]{0,1:T(8,128)(2,1)S(1)} %multiply_reduce_fusion), channel_id=1, replica_groups=mesh['req'=32,'mdl'=8] {'mdl'}, use_global_device_ids=true, to_apply=%region_4.5 | all-reduce | flops 12288 | bytes 49152 | tf_op jit(solution)/shard_map/psum | solution.py:58
  237.4 0.8 fusion.36
  238.2 0.2 convert_reduce_fusion
  238.4 0.8 and_bitcast_fusion
  239.2 0.1 select_reduce_fusion.3
  239.2 0.1 select_reduce_fusion.2
  239.3 0.1 select_reduce_fusion.1
  239.5 0.1 broadcast_multiply_fusion
  239.6 1.4 fusion.47
  241.0 2.1 fusion.51
  243.1 0.1 fusion.48
  243.2 0.3 fusion.14
  243.5 1.0 add_convert_fusion.3
  244.6 1.2 compare_and_fusion
  245.8 1.4 pad_add_fusion
  247.2 5.7 %gather_fusion.1 = bf16[24,2,224,128]{3,2,1,0:T(8,128)(2,1)} fusion(bf16[64,2,224,128]{3,2,1,0:T(8,128)(2,1)} %bitcast.70, s32[1024]{0:T(1024)S(1)} %pad_clamp_fusion), kind=kCustom, calls=%fused_computation.1 | custom fusion | bytes 5505120 | tf_op jit(solution)/shard_map/jit(_take)/gather | solution.py:104
  252.8 3.7 broadcast_select_fusion.1
  256.5 8.8 %copy.35 = bf16[24,2,224,128]{2,1,0,3:T(2,128)(2,1)} copy(bf16[24,2,224,128]{3,2,1,0:T(8,128)(2,1)} %broadcast_select_fusion.1) | data formatting | bytes 5505024 | tf_op jit(solution)/shard_map/jit(_take)/select_n | solution.py:104
  265.3 8.9 %gather_fusion.2 = bf16[24,2,224,64]{2,1,3,0:T(2,128)(2,1)S(1)} fusion(bf16[24,2,224,128]{2,1,0,3:T(2,128)(2,1)} %copy.35, s32[24]{0:T(128)S(1)} %get-tuple-element.24), kind=kCustom, calls=%fused_computation.2 | custom fusion | bytes 2752896 | tf_op jit(solution)/shard_map/vmap()/gather | solution.py:12
  274.2 6.5 %slice_reduce_fusion.1 = (bf16[24,64,224]{2,1,0:T(8,128)(2,1)S(1)}, bf16[24,64,224]{2,1,0:T(8,128)(2,1)S(1)}) fusion(bf16[24,64,2,224]{3,2,1,0:T(2,128)(2,1)S(1)} %bitcast.69), kind=kLoop, calls=%fused_computation.35 | loop fusion | bytes 2752512 | tf_op jit(solution)/shard_map/slice | solution.py:111
  280.7 0.4 concatenate.23
  281.1 0.6 copy.37
  281.7 0.4 concatenate.20
  282.1 0.6 copy.36
  282.7 0.0 copy-start.6
  282.8 9.7 %fusion.49 = (f32[2,768]{1,0:T(2,128)S(1)}, f32[2,768,2304]{2,1,0:T(8,128)}) fusion(pred[768,2304]{1,0:T(8,128)(4,1)} %pad_add_fusion, bf16[768,2,112]{0,2,1:T(8,128)(2,1)S(1)} %copy-done.7, bf16[1536,2,112]{0,2,1:T(8,128)(2,1)S(1)} %copy.37, bf16[768,2,112]{0,2,1:T(8,128)(2,1)S(1)} %bitcast.81), kind=kOutput, calls=%fused_computation.96 | convolution fusion | flops 808945920 | bytes 17307648 | tf_op jit(solution)/shard_map/sub | solution.py:129
  292.5 7.6 %fusion.20 = bf16[2,112,768]{2,1,0:T(8,128)(2,1)S(1)} fusion(f32[2,768,2304]{2,1,0:T(8,128)} %get-tuple-element.23, f32[2,768]{1,0:T(2,128)S(1)} %get-tuple-element.22, bf16[1536,2,112]{0,2,1:T(8,128)(2,1)S(1)} %copy.36, bf16[768,2,112]{0,2,1:T(8,128)(2,1)S(1)} %copy-done.6), kind=kOutput, calls=%fused_computation.36 | convolution fusion | flops 802037760 | bytes 15538176 | tf_op jit(solution)/shard_map/hts,shd->thd/dot_general | solution.py:132
  300.1 0.0 copy-start.10
  300.1 2.5 convolution_convert_fusion
  302.6 0.0 all-reduce.3.cloned.1.call-update
  302.6 0.0 reduce-scatter.2.cloned.1.call-start
  302.7 50.1 %all-to-all-done.1 = bf16[32,3,56,608]{3,2,1,0:T(8,128)(2,1)} async-done(((bf16[32,3,56,608]{3,2,1,0:T(8,128)(2,1)}), bf16[32,3,56,608]{3,2,1,0:T(8,128)(2,1)}, u32[]{:S(2)}, u32[]{:S(2)}) %all-to-all-start.1) | async-done | bytes 6537248 | tf_op jit(solution)/shard_map/all_to_all | solution.py:149
  352.8 5.9 %fusion.46 = (bf16[1,32,56,608]{3,2,0,1:T(8,128)(2,1)}, bf16[1,32,56,608]{3,2,0,1:T(8,128)(2,1)}, bf16[1,32,56,608]{3,2,0,1:T(8,128)(2,1)S(1)}) fusion(bf16[3,32,56,608]{3,2,0,1:T(8,128)(2,1)} %bitcast.26), kind=kLoop, calls=%fused_computation.93 | loop fusion | bytes 13074432 | tf_op jit(solution)/shard_map/slice | solution.py:152
  358.7 16.4 %all-reduce.3.cloned.1.call-done = bf16[768,1792]{1,0:T(8,128)(2,1)} async-done(((bf16[768,1792]{1,0:T(8,128)(2,1)}), bf16[768,1792]{1,0:T(8,128)(2,1)}) %all-reduce.3.cloned.1.call-update) | async-done | bytes 2752528 | tf_op jit(solution)/shard_map/psum | solution.py:142
  375.0 3.7 fusion.6
  378.7 3.4 fusion.25
  382.1 10.6 %convolution_convert_fusion.1 = bf16[768,1792]{1,0:T(8,128)(2,1)} fusion(bf16[1792,608]{1,0:T(8,128)(2,1)} %bitcast.76, f32[768,608]{0,1:T(8,128)} %fusion.25, bf16[1792,608]{1,0:T(8,128)(2,1)} %bitcast.75, bf16[768,1792]{1,0:T(8,128)(2,1)} %copy-done.2, f32[1792]{0:T(1024)S(1)} %convert_element_type.118, f32[768]{0:T(1024)S(1)} %add_rsqrt_fusion), kind=kOutput, calls=%fused_computation.22 | convolution fusion | flops 3356737536 | bytes 11741184 | tf_op jit(solution)/shard_map/tf,df->td/dot_general | solution.py:155
  392.7 0.0 reduce-scatter.2.cloned.1.call-update
  392.7 37.3 %reduce-scatter.2.cloned.1.call-done = bf16[96,1792]{1,0:T(8,128)(2,1)} async-done(((bf16[768,1792]{1,0:T(8,128)(2,1)}), bf16[96,1792]{1,0:T(8,128)(2,1)}) %reduce-scatter.2.cloned.1.call-update) | async-done | bytes 344080 | tf_op jit(solution)/shard_map/reduce_scatter | solution.py:159
  430.1 1.9 add_convert_fusion.1
  (42 shorter events, 0.3 us)
Async XLA Ops:
  6.5 197.1 %copy-start = (bf16[3,224,1792]{2,1,0:T(8,128)(2,1)S(1)}, bf16[3,224,1792]{2,1,0:T(8,128)(2,1)}, u32[]{:S(2)}) copy-start(bf16[3,224,1792]{2,1,0:T(8,128)(2,1)} %param.16) | copy-start | bytes 7225348
  19.4 174.6 %copy-start.8 = (bf16[3,56,608]{2,1,0:T(8,128)(2,1)S(1)}, bf16[3,56,608]{2,1,0:T(8,128)(2,1)}, u32[]{:S(2)}) copy-start(bf16[3,56,608]{2,1,0:T(8,128)(2,1)} %param.22) | copy-start | bytes 612868
  197.4 5.8 %copy-start.11 = (s32[1,24]{1,0:T(1,128)S(1)}, s32[1,24]{1,0:T(1,128)}, u32[]{:S(2)}) copy-start(s32[1,24]{1,0:T(1,128)} %param.25) | copy-start | bytes 292
  197.4 155.4 %all-to-all-start.1 = ((bf16[32,3,56,608]{3,2,1,0:T(8,128)(2,1)}), bf16[32,3,56,608]{3,2,1,0:T(8,128)(2,1)}, u32[]{:S(2)}, u32[]{:S(2)}) async-start(bf16[32,3,56,608]{3,2,1,0:T(8,128)(2,1)} %stack.2), calls=%async_computation.1 | async-start | bytes 13762560 | tf_op jit(solution)/shard_map/all_to_all | solution.py:149
  203.2 171.9 %all-reduce.3.cloned.1.call-start = ((), (), s32[]{:S(2)}) async-start(), calls=%async_computation.3 | async-start | bytes 5505024 | tf_op jit(solution)/shard_map/psum | solution.py:142
  203.7 5.4 %copy-start.9 = (s32[768]{0:T(1024)S(1)}, s32[768]{0:T(1024)}, u32[]{:S(2)}) copy-start(s32[768]{0:T(1024)} %param.24) | copy-start | bytes 9220
  203.7 5.4 %copy-start.5 = (bf16[8,1792,16]{1,2,0:T(8,128)(2,1)S(1)}, bf16[8,1792,16]{1,2,0:T(8,128)(2,1)}, u32[]{:S(2)}) copy-start(bf16[8,1792,16]{1,2,0:T(8,128)(2,1)} %param.18) | copy-start | bytes 1376260
  207.6 1.4 copy-start.3
  209.0 30.2 %copy-start.12 = (f32[4]{0:T(128)S(1)}, f32[4]{0:T(128)}, u32[]{:S(2)}) copy-start(f32[4]{0:T(128)} %param.20) | copy-start | bytes 52
  209.0 30.2 %copy-start.13 = (s32[24]{0:T(128)S(1)}, s32[24]{0:T(128)}, u32[]{:S(2)}) copy-start(s32[24]{0:T(128)} %param.26) | copy-start | bytes 292
  281.1 1.6 copy-start.7
  282.7 9.7 %copy-start.6 = (bf16[768,2,112]{0,2,1:T(8,128)(2,1)S(1)}, bf16[768,2,112]{0,2,1:T(8,128)(2,1)}, u32[]{:S(2)}) copy-start(bf16[768,2,112]{0,2,1:T(8,128)(2,1)} %get-tuple-element.20) | copy-start | bytes 1032196
  292.5 7.6 %copy-start.4 = (bf16[224,1792]{1,0:T(8,128)(2,1)S(1)}, bf16[224,1792]{1,0:T(8,128)(2,1)}, u32[]{:S(2)}) copy-start(bf16[224,1792]{1,0:T(8,128)(2,1)} %param.17) | copy-start | bytes 2408452
  300.1 2.6 copy-start.10
  302.6 127.5 %reduce-scatter.2.cloned.1.call-start = ((), (), s32[]{:S(2)}) async-start(), calls=%async_computation.4 | async-start | bytes 3096576 | tf_op jit(solution)/shard_map/reduce_scatter | solution.py:159
  378.7 3.4 copy-start.2
  382.1 49.9 %copy-start.1 = (bf16[3,224,1792]{2,1,0:T(8,128)(2,1)S(1)}, bf16[3,224,1792]{2,1,0:T(8,128)(2,1)}, u32[]{:S(2)}) copy-start(bf16[3,224,1792]{2,1,0:T(8,128)(2,1)} %param.16) | copy-start | bytes 7225348
Sparse Core Ops, SparseCore 0:
  302.7 72.2 all-reduce.2
  392.9 37.1 reduce-scatter.1
